TPU v7x, 512 devices: a whole 4x8x8 slice. The times are simulated.
512 devices in a mesh: dp: 8 (over y_hi, core), mp: 64 (over z, x, y_lo).
Axes of the slice: x: 4, y: 8 (y_hi: 4, y_lo: 2; y = y_hi * 2 + y_lo), z: 8, core: 2. Of those that a mesh axis runs over, the one named last changes fastest.
Arguments:
- queries: bfloat16 [65536, 768], P(('dp', 'mp')), may hold values from -30 to 30
- first_owner: int32 [65536, 1], P(('dp', 'mp')), may hold values from 0 to 63; in each aligned block of 128 rows (0 to 127, 128 to 255, ...) at most 4 rows name the same one
- first_row: int32 [65536], P(('dp', 'mp')), may hold values from 0 to 255
- tool_table: bfloat16 [16384, 768], P('mp'), may hold values from -6 to 6
- norm_gain: bfloat16 [768], replicated, may hold values from 0.25 to 1.75
- weight_in: bfloat16 [3072, 768], P('mp'), may hold values from -0.21875 to 0.21875
- bias_in: bfloat16 [3072], P('mp'), may hold values from -3 to 3
- weight_out: bfloat16 [3072, 768], P('mp'), may hold values from -0.109375 to 0.109375
- bias_out: bfloat16 [768], replicated, may hold values from -3 to 3
- tool_embeds: bfloat16 [512, 768], P('dp'), may hold values from -2 to 2
- positive: int32 [65536], P(('dp', 'mp')), may hold values from 0 to 511
Outputs:
- updated: bfloat16 [65536, 768], P(('dp', 'mp'))
- chain_loss: float32 [65536], P(('dp', 'mp'))
- query_grad: float32 [65536, 768], P(('dp', 'mp'))
- tool_grad: float32 [512, 768], P('dp')
Inputs may be any that keep to these rules, and one draw needn't show every extreme that they name: `first_owner`: among the 128 chains of one device at most 4 name the same owner, a bound that some block reaches of them.
All inputs are finite; a program needn't handle non-finite values.
Results may differ from a plain program's by a relative error of at most 0.0078.
Values may be sent and summed in bfloat16 or wider, within the bound.
A program may use at most 64 MiB of HBM per device.

v0:
```python
import jax
import jax.numpy as jnp
import numpy as np
from jax import lax
from jax.sharding import PartitionSpec as P


def from_behind(block, axis, distance):
    devices = range(lax.axis_size(axis))
    route = [((i - distance) % len(devices), i) for i in devices]
    return lax.ppermute(block, axis, route)


def layer_normed(combined, norm_gain):
    row_mean = jnp.mean(combined, axis=1, keepdims=True)
    centred = combined - row_mean
    spread = jnp.mean(centred * centred, axis=1, keepdims=True)
    return (centred * lax.rsqrt(spread + 1e-05) * norm_gain.astype(jnp.float32)[None, :]).astype(
        jnp.bfloat16
    )


def hidden_terms(pieces, normed):
    in_piece, bias_piece, out_piece = pieces
    preact = lax.dot_general(
        normed, in_piece, (((1,), (1,)), ((), ())), preferred_element_type=jnp.float32
    )
    preact = preact + bias_piece.astype(jnp.float32)[None, :]
    activated = jax.nn.gelu(preact, approximate=True).astype(jnp.bfloat16)
    return jnp.dot(activated, out_piece, preferred_element_type=jnp.float32)


def local(
    queries,
    first_owner,
    first_row,
    tool_table,
    norm_gain,
    weight_in,
    bias_in,
    weight_out,
    bias_out,
    tool_embeds,
    positive,
):
    chain_count, feature_count = queries.shape
    groups = lax.axis_size("mp")
    cycle_size = lax.axis_size("dp")
    cycle_index = lax.axis_index("dp")
    capacity = 2 * chain_count // groups
    owner_ids = first_owner[:, 0]
    owner_marks = (owner_ids[:, None] == jnp.arange(groups, dtype=jnp.int32)[None, :]).astype(
        jnp.int32
    )
    rank_in_owner = jnp.sum((jnp.cumsum(owner_marks, axis=0) - owner_marks) * owner_marks, axis=1)
    slot_index = owner_ids * capacity + rank_in_owner
    request = (
        jnp.zeros((groups * capacity,), jnp.int32)
        .at[slot_index]
        .set(first_row)
        .reshape(groups, capacity)
    )
    table_rows = jnp.take(
        tool_table, lax.all_to_all(request, "mp", split_axis=0, concat_axis=0, tiled=True), axis=0
    )
    fetched = lax.all_to_all(table_rows, "mp", split_axis=0, concat_axis=0, tiled=True)
    first_rows = fetched.reshape(groups * capacity, feature_count)[slot_index]
    combined = queries.astype(jnp.float32) + first_rows.astype(jnp.float32)
    normed = layer_normed(combined, norm_gain)
    branch_sum = hidden_terms(
        (
            lax.all_gather(weight_in, "mp", axis=0, tiled=True),
            lax.all_gather(bias_in, "mp", axis=0, tiled=True),
            lax.all_gather(weight_out, "mp", axis=0, tiled=True),
        ),
        normed,
    )
    updated = (combined + branch_sum + bias_out.astype(jnp.float32)[None, :]).astype(jnp.bfloat16)
    block_rows = tool_embeds.shape[0]
    forward_hops = cycle_size - 1
    block_list = [tool_embeds]
    offset_list = [0]
    visiting = tool_embeds
    for hop_number in range(forward_hops):
        visiting = from_behind(visiting, "dp", 1)
        block_list.append(visiting)
        offset_list.append(hop_number + 1)
    all_tools = jnp.concatenate(block_list, axis=0)
    block_owner = (cycle_index - jnp.asarray(offset_list, jnp.int32)) % cycle_size
    column_ids = (
        block_owner[:, None] * block_rows + jnp.arange(block_rows, dtype=jnp.int32)[None, :]
    ).reshape(-1)
    scores = lax.dot_general(
        updated, all_tools, (((1,), (1,)), ((), ())), preferred_element_type=jnp.float32
    )
    row_max = jnp.max(scores, axis=1, keepdims=True)
    log_total = row_max + jnp.log(jnp.sum(jnp.exp(scores - row_max), axis=1, keepdims=True))
    is_positive = (column_ids[None, :] == positive[:, None]).astype(jnp.float32)
    chain_loss = log_total[:, 0] - jnp.sum(scores * is_positive, axis=1)
    weights_grad = (jnp.exp(scores - log_total) - is_positive).astype(jnp.bfloat16)
    query_grad = jnp.dot(weights_grad, all_tools, preferred_element_type=jnp.float32)
    position_of = np.zeros((cycle_size,), np.int32)
    for list_index, offset_value in enumerate(offset_list):
        position_of[offset_value] = list_index

    def block_term(offset_value):
        list_index = int(position_of[offset_value])
        columns = weights_grad[:, list_index * block_rows : (list_index + 1) * block_rows]
        return lax.dot_general(
            columns, updated, (((0,), (0,)), ((), ())), preferred_element_type=jnp.float32
        )

    partial_grad = jnp.zeros((block_rows, feature_count), jnp.float32)
    for hop_number in range(cycle_size - 1):
        partial_grad = partial_grad + block_term(hop_number + 1)
        partial_grad = from_behind(partial_grad.astype(jnp.bfloat16), "dp", 1).astype(
            partial_grad.dtype
        )
    partial_grad = partial_grad + block_term(0)
    grad_scale = (block_rows * cycle_size / (chain_count * groups * cycle_size)) ** 0.5
    tool_grad = lax.psum(partial_grad, "mp") * grad_scale
    return (updated, chain_loss, query_grad, tool_grad)


def solution(mesh):
    in_specs = (
        P(("dp", "mp"), None),
        P(("dp", "mp"), None),
        P(("dp", "mp")),
        P("mp", None),
        P(),
        P("mp", None),
        P("mp"),
        P("mp", None),
        P(),
        P("dp", None),
        P(("dp", "mp")),
    )
    out_specs = (P(("dp", "mp"), None), P(("dp", "mp")), P(("dp", "mp"), None), P("dp", None))
    return jax.shard_map(local, mesh=mesh, in_specs=in_specs, out_specs=out_specs, check_vma=False)
```

profile of v0, /device:TPU:16, one launch (start us, length us, event | category | flops | bytes accessed | tf_op | source)
XLA Modules:
  0.0 1266.2 jit_solution(13888815105655201328)
XLA Ops:
  12.9 14.8 %all-to-all-start = ((s32[64,1,4]{2,1,0:T(1,128)}), s32[64,1,4]{2,1,0:T(1,128)S(1)}, u32[]{:S(2)}, u32[]{:S(2)}) async-start(s32[64,1,4]{2,1,0:T(1,128)} %bitcast.3), calls=%async_computation | async-start | bytes 65536 | tf_op jit(solution)/shard_map/all_to_all | solution.py:64
  27.7 1.9 collective-permute-start
  33.4 163.7 %all-reduce = bf16[3072]{0:T(1024)(128)(2,1)S(1)} all-reduce(bf16[3072]{0:T(1024)(128)(2,1)S(1)} %dynamic-update-slice), channel_id=1, replica_groups=mesh['dp'=8,'mp'=64] {'mp'}, use_global_device_ids=true, to_apply=%add | all-reduce | flops 3072 | bytes 12288
  201.1 5.3 all-to-all-start.1
  206.5 1.9 collective-permute-start.1
  208.5 6.4 collective-permute-done.1
  214.9 2.1 collective-permute-start.2
  217.0 7.5 collective-permute-done.2
  226.4 6.5 collective-permute-done.3
  234.8 5.5 collective-permute-done.4
  240.3 4.1 collective-permute-start.5
  244.4 4.4 collective-permute-done.5
  248.8 3.8 collective-permute-start.6
  252.7 5.0 collective-permute-done.6
  259.1 72.0 %all-gather.3.cloned.1.call-done = bf16[3072,768]{1,0:T(8,128)(2,1)} async-done(((bf16[48,768]{1,0:T(8,128)(2,1)}), bf16[3072,768]{1,0:T(8,128)(2,1)}) %all-gather.3.cloned.1.call-update) | async-done | bytes 4718608 | tf_op jit(solution)/shard_map/all_gather | solution.py:72
  331.1 314.4 %all-gather.5.cloned.1.call-done = bf16[3072,768]{1,0:T(8,128)(2,1)} async-done(((bf16[48,768]{1,0:T(8,128)(2,1)}), bf16[3072,768]{1,0:T(8,128)(2,1)}) %all-gather.5.cloned.1.call-update) | async-done | bytes 4718608 | tf_op jit(solution)/shard_map/all_gather | solution.py:74
  645.5 6.2 fusion.9
  653.4 1.9 collective-permute-start.7
  655.3 5.7 collective-permute-done.7
  661.2 1.9 collective-permute-start.8
  663.4 5.7 collective-permute-done.8
  669.1 1.9 collective-permute-start.9
  671.2 5.8 collective-permute-done.9
  677.0 1.9 collective-permute-start.10
  679.2 5.7 collective-permute-done.10
  684.9 2.1 collective-permute-start.11
  687.2 4.6 collective-permute-done.11
  691.8 3.3 collective-permute-start.12
  695.3 3.3 collective-permute-done.12
  698.6 4.5 collective-permute-start.13
  703.3 2.2 collective-permute-done.13
  707.2 550.8 %all-reduce.3.cloned.1.call-done = f32[64,768]{1,0:T(8,128)} async-done(((f32[64,768]{1,0:T(8,128)}), f32[64,768]{1,0:T(8,128)}) %all-reduce.3.cloned.1.call-update) | async-done | bytes 196624 | tf_op jit(solution)/shard_map/psum | solution.py:121
  (76 shorter events, 24.5 us)
Async XLA Ops:
  7.2 191.6 %copy-start = (bf16[256,768]{1,0:T(8,128)(2,1)S(1)}, bf16[256,768]{1,0:T(8,128)(2,1)}, u32[]{:S(2)}) copy-start(bf16[256,768]{1,0:T(8,128)(2,1)} %param.15) | copy-start | bytes 1179652
  7.2 323.9 %all-gather.3.cloned.1.call-start = ((), (), s32[]{:S(2)}) async-start(), calls=%async_computation.2 | async-start | bytes 4792320 | tf_op jit(solution)/shard_map/all_gather | solution.py:72
  7.9 637.6 %all-gather.5.cloned.1.call-start = ((), (), s32[]{:S(2)}) async-start(), calls=%async_computation.3 | async-start | bytes 4792320 | tf_op jit(solution)/shard_map/all_gather | solution.py:74
  12.9 185.7 %all-to-all-start = ((s32[64,1,4]{2,1,0:T(1,128)}), s32[64,1,4]{2,1,0:T(1,128)S(1)}, u32[]{:S(2)}, u32[]{:S(2)}) async-start(s32[64,1,4]{2,1,0:T(1,128)} %bitcast.3), calls=%async_computation | async-start | bytes 65536 | tf_op jit(solution)/shard_map/all_to_all | solution.py:64
  27.7 178.8 %collective-permute-start = (bf16[64,768]{1,0:T(8,128)(2,1)}, bf16[64,768]{1,0:T(8,128)(2,1)S(1)}, u32[]{:S(2)}, u32[]{:S(2)}) collective-permute-start(bf16[64,768]{1,0:T(8,128)(2,1)} %param.21), channel_id=1, source_target_pairs={{448,0},{0,64},{64,128},{128,192},{192,256},{256,320},{320,384},{3... | collective-permute-start | bytes 294920 | tf_op jit(solution)/shard_map/ppermute | solution.py:11
  201.1 56.6 %all-to-all-start.1 = ((bf16[64,4,768]{2,1,0:T(4,128)(2,1)}), bf16[64,4,768]{2,1,0:T(4,128)(2,1)S(1)}, u32[]{:S(2)}, u32[]{:S(2)}) async-start(bf16[64,4,768]{2,1,0:T(4,128)(2,1)} %broadcast_select_fusion), calls=%async_computation.1 | async-start | bytes 786432 | tf_op jit(solution)/shard_map/all_to_all | solution.py:66
  206.5 1051.5 %all-reduce.3.cloned.1.call-start = ((), (), s32[]{:S(2)}) async-start(), calls=%async_computation.4 | async-start | bytes 393216 | tf_op jit(solution)/shard_map/psum | solution.py:121
  206.5 8.4 collective-permute-start.1
  214.9 9.5 collective-permute-start.2
  224.4 8.4 collective-permute-start.3
  232.9 7.4 collective-permute-start.4
  234.8 23.9 %copy-start.2 = (bf16[128,768]{1,0:T(8,128)(2,1)S(1)}, bf16[128,768]{1,0:T(8,128)(2,1)}, u32[]{:S(2)}) copy-start(bf16[128,768]{1,0:T(8,128)(2,1)} %param.12) | copy-start | bytes 589828
  240.3 8.5 collective-permute-start.5
  248.8 8.9 collective-permute-start.6
  259.0 393.2 %copy-start.3 = (s32[128]{0:T(128)S(1)}, s32[128]{0:T(128)}, u32[]{:S(2)}) copy-start(s32[128]{0:T(128)} %param.22) | copy-start | bytes 1540
  651.7 51.4 %copy-start.1 = (bf16[128,768]{1,0:T(8,128)(2,1)}, bf16[128,768]{1,0:T(8,128)(2,1)S(1)}, u32[]{:S(2)}) copy-start(bf16[128,768]{1,0:T(8,128)(2,1)S(1)} %fusion.9) | copy-start | bytes 589828
  653.4 7.6 collective-permute-start.7
  661.2 7.9 collective-permute-start.8
  669.1 7.9 collective-permute-start.9
  677.0 7.9 collective-permute-start.10
  684.9 6.8 collective-permute-start.11
  691.8 6.8 collective-permute-start.12
  698.6 6.8 collective-permute-start.13
Sparse Core Ops, SparseCore 0:
  10.1 320.9 all-gather.2
  333.2 312.3 all-gather.4
  706.3 551.6 all-reduce.2
where the time goes:
time: 1270 us
  waiting for transfers between devices  1010 us (80%)
  blocking collectives  164 us (13%)
  starting transfers between devices  55.3 us (4%)
  between operations  14.9 us (1%)
    psum x1, waiting for transfers between devices, local(): tool_grad = lax.psum(partial_grad, 'mp') * grad_scale  551 us
    all_gather x1, waiting for transfers between devices, local(): lax.all_gather(weight_out, 'mp', axis=0, tiled=True)  314 us
    unnamed x1, blocking collectives  164 us
    all_gather x1, waiting for transfers between devices, local(): lax.all_gather(weight_in, 'mp', axis=0, tiled=True)  72 us
    ppermute x14, waiting for transfers between devices, from_behind(): return lax.ppermute(block, axis, route)  68.2 us
    ppermute x14, starting transfers between devices, from_behind(): return lax.ppermute(block, axis, route)  35.1 us
  transfers between devices with their start and end apart: 19, of which 16 were waited for; matrix products, arithmetic and copies ran while one was open for 1% of the time, Pallas kernels for 0%

commit v1 on v0

--- a/solution.py
+++ b/solution.py
@@ -69,7 +69,9 @@
     normed = layer_normed(combined, norm_gain)
     branch_sum = hidden_terms(
         (
-            lax.all_gather(weight_in, "mp", axis=0, tiled=True),
+            jnp.concatenate(
+                lax.all_to_all(jnp.stack([weight_in] * lax.axis_size("mp")), "mp", 0, 0), axis=0
+            ),
             lax.all_gather(bias_in, "mp", axis=0, tiled=True),
             lax.all_gather(weight_out, "mp", axis=0, tiled=True),
         ),

time: 1270 us -> 1010 us (0.80)
  waiting for transfers between devices: 1010 us -> 641 us
  blocking collectives: 164 us -> 267 us
    all_gather x1, waiting for transfers between devices: 314 us -> 49.5 us  [local(): lax.all_gather(weight_out, 'mp', axis=0, tiled=True)]
    all_gather x1 -> x0, waiting for transfers between devices: 72 us -> none  [local(): lax.all_gather(weight_in, 'mp', axis=0, tiled=True)]
    unnamed x1, blocking collectives: 164 us -> 223 us
    all_to_all x0 -> x2, blocking collectives: none -> 43.4 us  [the longest x1 25 us: local(): lax.all_to_all(request, 'mp', split_axis=0, concat_axis=0, tiled=True)]
    ppermute x14, waiting for transfers between devices: 68.2 us -> 38.1 us  [from_behind(): return lax.ppermute(block, axis, route)]
    ppermute x14, starting transfers between devices: 35.1 us -> 59.7 us  [from_behind(): return lax.ppermute(block, axis, route)]
    all_to_all x2 -> x1, starting transfers between devices: 20.1 us -> 5.83 us  [local(): lax.all_to_all(jnp.stack([weight_in] * lax.axis_size('mp')), 'mp', 0, 0)]
  transfers between devices with their start and end apart: 19 -> 17, of which waited for: 16 -> 15; matrix products, arithmetic and copies ran while one was open for 1% -> 1% of each run, Pallas kernels for 0% -> 0%
where the time goes in v1:
time: 1010 us
  waiting for transfers between devices  641 us (63%)
  blocking collectives  267 us (26%)
  starting transfers between devices  65.6 us (6%)
  between operations  15.2 us (2%)
    psum x1, waiting for transfers between devices, local(): tool_grad = lax.psum(partial_grad, 'mp') * grad_scale  553 us
    unnamed x1, blocking collectives  223 us
    ppermute x14, starting transfers between devices, from_behind(): return lax.ppermute(block, axis, route)  59.7 us
    all_gather x1, waiting for transfers between devices, local(): lax.all_gather(weight_out, 'mp', axis=0, tiled=True)  49.5 us
    ppermute x14, waiting for transfers between devices, from_behind(): return lax.ppermute(block, axis, route)  38.1 us
    all_to_all x1, blocking collectives, local(): lax.all_to_all(request, 'mp', split_axis=0, concat_axis=0, tiled=True)  25 us
  transfers between devices with their start and end apart: 17, of which 15 were waited for; matrix products, arithmetic and copies ran while one was open for 1% of the time, Pallas kernels for 0%

profile of v1, /device:TPU:16, one launch (start us, length us, event | category | flops | bytes accessed | tf_op | source)
XLA Modules:
  0.0 1012.6 jit_solution(16988291936560571691)
XLA Ops:
  10.9 25.0 %all_to_all.25 = s32[64,1,4]{2,1,0:T(1,128)S(1)} all-to-all(s32[64,1,4]{2,1,0:T(1,128)S(1)} %bitcast.30), channel_id=1, replica_groups=mesh['dp'=8,'mp'=64] {'mp'}, dimensions={0} | all-to-all | bytes 2048 | tf_op jit(solution)/shard_map/all_to_all | solution.py:64
  37.6 18.4 %all_to_all.26 = bf16[64,4,768]{2,1,0:T(4,128)(2,1)S(1)} all-to-all(bf16[64,4,768]{2,1,0:T(4,128)(2,1)S(1)} %broadcast_select_fusion), channel_id=1, replica_groups=mesh['dp'=8,'mp'=64] {'mp'}, dimensions={0} | all-to-all | bytes 786432 | tf_op jit(solution)/shard_map/all_to_all | solution.py:66
  56.0 2.5 stack.2
  58.6 5.8 all-to-all-start.2
  65.2 1.9 collective-permute-start
  69.3 223.4 %all-reduce = bf16[3072]{0:T(1024)(128)(2,1)S(1)} all-reduce(bf16[3072]{0:T(1024)(128)(2,1)S(1)} %dynamic-update-slice), channel_id=1, replica_groups=mesh['dp'=8,'mp'=64] {'mp'}, use_global_device_ids=true, to_apply=%add | all-reduce | flops 3072 | bytes 12288
  293.0 1.9 collective-permute-start.1
  294.9 4.9 collective-permute-done.1
  299.8 1.9 collective-permute-start.2
  301.8 6.0 collective-permute-done.2
  307.8 2.8 collective-permute-start.3
  310.5 5.0 collective-permute-done.3
  315.5 3.6 collective-permute-start.4
  319.1 3.6 collective-permute-done.4
  322.7 4.6 collective-permute-start.5
  327.4 3.2 collective-permute-done.5
  330.6 6.5 collective-permute-start.6
  337.1 2.0 collective-permute-done.6
  340.4 49.5 %all-gather.2.cloned.1.call-done = bf16[3072,768]{1,0:T(8,128)(2,1)} async-done(((bf16[48,768]{1,0:T(8,128)(2,1)}), bf16[3072,768]{1,0:T(8,128)(2,1)}) %all-gather.2.cloned.1.call-update) | async-done | bytes 4718608 | tf_op jit(solution)/shard_map/all_gather | solution.py:76
  389.9 6.2 fusion.9
  397.7 1.9 collective-permute-start.7
  399.7 4.9 collective-permute-done.7
  404.8 3.1 collective-permute-start.8
  408.2 3.5 collective-permute-done.8
  411.7 4.5 collective-permute-start.9
  416.3 2.2 collective-permute-done.9
  418.5 5.8 collective-permute-start.10
  425.4 7.0 collective-permute-start.11
  433.3 7.1 collective-permute-start.12
  441.4 7.1 collective-permute-start.13
  451.2 552.9 %all-reduce.3.cloned.1.call-done = f32[64,768]{1,0:T(8,128)} async-done(((f32[64,768]{1,0:T(8,128)}), f32[64,768]{1,0:T(8,128)}) %all-reduce.3.cloned.1.call-update) | async-done | bytes 196624 | tf_op jit(solution)/shard_map/psum | solution.py:123
  1004.1 1.6 broadcast_multiply_fusion
  (84 shorter events, 17.1 us)
Async XLA Ops:
  7.2 28.9 %copy-start = (bf16[256,768]{1,0:T(8,128)(2,1)S(1)}, bf16[256,768]{1,0:T(8,128)(2,1)}, u32[]{:S(2)}) copy-start(bf16[256,768]{1,0:T(8,128)(2,1)} %param.15) | copy-start | bytes 1179652
  37.2 18.8 %copy-start.4 = (bf16[48,768]{1,0:T(8,128)(2,1)S(1)}, bf16[48,768]{1,0:T(8,128)(2,1)}, u32[]{:S(2)}) copy-start(bf16[48,768]{1,0:T(8,128)(2,1)} %param.17) | copy-start | bytes 221188
  58.6 6.6 copy-start.3
  58.6 10.5 %copy-start.8 = (bf16[48]{0:T(256)(128)(2,1)S(1)}, bf16[48]{0:T(256)(128)(2,1)}, u32[]{:S(2)}) copy-start(bf16[48]{0:T(256)(128)(2,1)} %param.18) | copy-start | bytes 292
  58.6 234.2 %copy-start.6 = (bf16[768]{0:T(1024)(128)(2,1)S(1)}, bf16[768]{0:T(1024)(128)(2,1)}, u32[]{:S(2)}) copy-start(bf16[768]{0:T(1024)(128)(2,1)} %param.16) | copy-start | bytes 4612
  58.6 234.2 %copy-start.7 = (bf16[768]{0:T(1024)(128)(2,1)S(1)}, bf16[768]{0:T(1024)(128)(2,1)}, u32[]{:S(2)}) copy-start(bf16[768]{0:T(1024)(128)(2,1)} %param.20) | copy-start | bytes 4612
  58.6 281.8 %all-to-all-start.2 = ((bf16[64,48,768]{2,1,0:T(8,128)(2,1)}), bf16[64,48,768]{2,1,0:T(8,128)(2,1)}, u32[]{:S(2)}, u32[]{:S(2)}) async-start(bf16[64,48,768]{2,1,0:T(8,128)(2,1)} %stack.2), calls=%async_computation.2 | async-start | bytes 9437184 | tf_op jit(solution)/shard_map/all_to_all | solution.py:73
  64.4 325.5 %all-gather.2.cloned.1.call-start = ((), (), s32[]{:S(2)}) async-start(), calls=%async_computation.3 | async-start | bytes 4792320 | tf_op jit(solution)/shard_map/all_gather | solution.py:76
  65.2 939.0 %all-reduce.3.cloned.1.call-start = ((), (), s32[]{:S(2)}) async-start(), calls=%async_computation.4 | async-start | bytes 393216 | tf_op jit(solution)/shard_map/psum | solution.py:123
  65.2 227.8 %collective-permute-start = (bf16[64,768]{1,0:T(8,128)(2,1)S(1)}, bf16[64,768]{1,0:T(8,128)(2,1)S(1)}, u32[]{:S(2)}, u32[]{:S(2)}) collective-permute-start(bf16[64,768]{1,0:T(8,128)(2,1)S(1)} %copy-done.3), channel_id=1, source_target_pairs={{448,0},{0,64},{64,128},{128,192},{192,256},{256,320},{320,384},{3... | collective-permute-start | bytes 294920 | tf_op jit(solution)/shard_map/ppermute | solution.py:11
  293.0 6.8 collective-permute-start.1
  299.8 7.9 collective-permute-start.2
  307.8 7.8 collective-permute-start.3
  315.5 7.2 collective-permute-start.4
  319.1 20.9 %copy-start.2 = (bf16[128,768]{1,0:T(8,128)(2,1)S(1)}, bf16[128,768]{1,0:T(8,128)(2,1)}, u32[]{:S(2)}) copy-start(bf16[128,768]{1,0:T(8,128)(2,1)} %param.12) | copy-start | bytes 589828
  322.7 7.8 collective-permute-start.5
  330.6 8.5 collective-permute-start.6
  389.9 6.7 copy-start.5
  396.1 52.4 %copy-start.1 = (bf16[128,768]{1,0:T(8,128)(2,1)}, bf16[128,768]{1,0:T(8,128)(2,1)S(1)}, u32[]{:S(2)}) copy-start(bf16[128,768]{1,0:T(8,128)(2,1)S(1)} %fusion.9) | copy-start | bytes 589828
  397.7 6.9 collective-permute-start.7
  404.8 6.8 collective-permute-start.8
  411.7 6.8 collective-permute-start.9
  418.5 6.8 collective-permute-start.10
  425.4 7.9 collective-permute-start.11
  433.3 8.0 collective-permute-start.12
  441.4 8.0 collective-permute-start.13
Sparse Core Ops, SparseCore 0:
  67.3 322.5 all-gather.1
  450.3 553.8 all-reduce.2
